TPU v7x, 256 devices: a whole 4x4x8 slice. The times are simulated.
256 devices in a mesh: dp: 64 (over z, x, y_hi), tensor: 4 (over y_lo, core).
Axes of the slice: x: 4, y: 4 (y_hi: 2, y_lo: 2; y = y_hi * 2 + y_lo), z: 8, core: 2. Of those that a mesh axis runs over, the one named last changes fastest.
Arguments:
- inputs: float32 [64, 197, 768], P('dp')
- cotangent: float32 [64, 197, 768], P('dp'), may hold values from -6 to 6
- norm_gains: float32 [2, 768], P(None, 'dp'), may hold values from 0.5 to 1.5
- attn_mats: float32 [4, 768, 768], P(None, 'dp', 'tensor')
- router: float32 [768, 3], P('dp'), may hold values from -0.4375 to 0.4375
- expert_in: float32 [3, 768, 1536], P(None, 'dp', 'tensor'), may hold values from -0.21875 to 0.21875
- expert_out: float32 [3, 768, 1536], P(None, 'dp', 'tensor'), may hold values from -0.3125 to 0.3125
- moment_gains: float32 [2, 768], P(None, 'dp'), may hold values from -128 to 128
- moment_attn: float32 [4, 768, 768], P(None, 'dp', 'tensor'), may hold values from -32 to 32
- moment_router: float32 [768, 3], P('dp'), may hold values from -320 to 320
- moment_in: float32 [3, 768, 1536], P(None, 'dp', 'tensor'), may hold values from -32 to 32
- moment_out: float32 [3, 768, 1536], P(None, 'dp', 'tensor'), may hold values from -32 to 32
- routes: int32 [64, 197, 2], P('dp'), may hold values from 0 to 2, all different within a row; in each aligned block of 197 rows (0 to 196, 197 to 393, ..., all dimensions but the last counted through in order) at most 197 rows name the same one
Outputs:
- output: float32 [64, 197, 768], P('dp')
- grad_inputs: float32 [64, 197, 768], P('dp')
- grad_gains: float32 [2, 768], P(None, 'dp')
- grad_attn: float32 [4, 768, 768], P(None, 'dp', 'tensor')
- grad_router: float32 [768, 3], P('dp')
- grad_in: float32 [3, 768, 1536], P(None, 'dp', 'tensor')
- grad_out: float32 [3, 768, 1536], P(None, 'dp', 'tensor')
- gains_new: float32 [2, 768], P(None, 'dp')
- attn_new: float32 [4, 768, 768], P(None, 'dp', 'tensor')
- router_new: float32 [768, 3], P('dp')
- in_new: float32 [3, 768, 1536], P(None, 'dp', 'tensor')
- out_new: float32 [3, 768, 1536], P(None, 'dp', 'tensor')
- moment_gains_new: float32 [2, 768], P(None, 'dp')
- moment_attn_new: float32 [4, 768, 768], P(None, 'dp', 'tensor')
- moment_router_new: float32 [768, 3], P('dp')
- moment_in_new: float32 [3, 768, 1536], P(None, 'dp', 'tensor')
- moment_out_new: float32 [3, 768, 1536], P(None, 'dp', 'tensor')
Inputs may be any that keep to these rules, and one draw needn't show every extreme that they name: `routes`: in the rows of one index of dp no expert is named by more than 197 of them, a bound that some block reaches; a row's two experts differ.
All inputs are finite; a program needn't handle non-finite values.
Results may differ from a plain program's by a relative error of at most 0.025.
The roundings to bfloat16 on the way count: a program that leaves them out, or rounds other values in their place, can miss the bound.
Values may be sent and summed in bfloat16 or wider, within the bound.
A program may use at most 128 MiB of HBM per device.

v0:
```python
import math
import jax
import jax.numpy as jnp
import numpy as np
from jax import lax
from jax.sharding import PartitionSpec as P

HEAD_DIM = 64
EF = 3
NS_ITERS = 3
CAP = 197
EPSILON = 1e-06
MOMENTUM = 0.9
MUON_RATE = 0.5
SMALL_RATE = 0.5
NEWTON_A = 3.4445
NEWTON_B = -4.775
NEWTON_C = 2.0315
ROOT_HALF = 0.7071067811865476
INV_ROOT_TAU = 0.3989422804014327


def for_sending(value):
    return jax.tree.map(lambda a: a.astype(jnp.bfloat16) if a.dtype == jnp.float32 else a, value)


def round_half(operand):
    return operand.astype(jnp.bfloat16)


def settle(operand):
    return lax.optimization_barrier(operand.astype(jnp.bfloat16))


def to_single(operand):
    return operand.astype(jnp.float32)


def contract_rows(left_mat, right_mat):
    return lax.dot_general(
        left_mat, right_mat, (((0,), (0,)), ((), ())), preferred_element_type=jnp.float32
    )


def contract_cols(left_mat, right_mat):
    return lax.dot_general(
        left_mat, right_mat, (((1,), (1,)), ((), ())), preferred_element_type=jnp.float32
    )


def fold_sources(received, source_count):
    return jnp.sum(
        received.reshape((source_count, received.shape[0] // source_count) + received.shape[1:]),
        axis=0,
    )


def norm_forward(row_data, gain_row):
    center = row_data - jnp.mean(row_data, axis=-1, keepdims=True)
    inv_std = lax.rsqrt(jnp.mean(center * center, axis=-1, keepdims=True) + EPSILON)
    normal = center * inv_std
    return (normal, inv_std, round_half(normal * gain_row))


def norm_backward(grad_result, normal, inv_std, gain_row):
    scaled = grad_result * gain_row
    grad_data = inv_std * (
        scaled
        - jnp.mean(scaled, axis=-1, keepdims=True)
        - normal * jnp.mean(scaled * normal, axis=-1, keepdims=True)
    )
    return (grad_data, jnp.sum(grad_result * normal, axis=0))


def gelu_value(pre_act):
    return 0.5 * pre_act * (1.0 + lax.erf(pre_act * ROOT_HALF))


def gelu_slope(pre_act):
    return 0.5 * (1.0 + lax.erf(pre_act * ROOT_HALF)) + pre_act * INV_ROOT_TAU * jnp.exp(
        -0.5 * pre_act * pre_act
    )


def score_table(queries, key_rows):
    return jnp.einsum("bqhd,bkhd->bhqk", queries, key_rows, preferred_element_type=jnp.float32) * (
        1.0 / math.sqrt(HEAD_DIM)
    )


def attention_forward(normed, mats_half, image_count, seq_len):
    head_count = mats_half.shape[2] // HEAD_DIM

    def project(which_mat):
        return round_half(
            jnp.dot(normed, mats_half[which_mat], preferred_element_type=jnp.float32)
        ).reshape(image_count, seq_len, head_count, HEAD_DIM)

    queries = project(0)
    key_rows = project(1)
    value_rows = project(2)
    scores = score_table(queries, key_rows)
    row_peak = jnp.max(scores, axis=-1, keepdims=True)
    log_total = row_peak + jnp.log(jnp.sum(jnp.exp(scores - row_peak), axis=-1, keepdims=True))
    prob_half = round_half(jnp.exp(scores - log_total))
    attn_rows = round_half(
        jnp.einsum("bhqk,bkhd->bqhd", prob_half, value_rows, preferred_element_type=jnp.float32)
    )
    return (
        queries,
        key_rows,
        value_rows,
        log_total,
        attn_rows.reshape(image_count * seq_len, head_count * HEAD_DIM),
    )


def attention_backward(grad_attn_rows, queries, key_rows, value_rows, log_total):
    image_count, seq_len, head_count, head_size = queries.shape
    grad_heads = grad_attn_rows.reshape(image_count, seq_len, head_count, head_size)
    prob_full = jnp.exp(score_table(queries, key_rows) - log_total)
    prob_half = round_half(prob_full)
    grad_prob = jnp.einsum(
        "bqhd,bkhd->bhqk", grad_heads, value_rows, preferred_element_type=jnp.float32
    )
    grad_values = round_half(
        jnp.einsum("bhqk,bqhd->bkhd", prob_half, grad_heads, preferred_element_type=jnp.float32)
    )
    spread = jnp.sum(prob_full * grad_prob, axis=-1, keepdims=True)
    grad_scores = round_half(prob_full * (grad_prob - spread) * (1.0 / math.sqrt(HEAD_DIM)))
    grad_queries = round_half(
        jnp.einsum("bhqk,bkhd->bqhd", grad_scores, key_rows, preferred_element_type=jnp.float32)
    )
    grad_keys = round_half(
        jnp.einsum("bhqk,bqhd->bkhd", grad_scores, queries, preferred_element_type=jnp.float32)
    )
    row_total = image_count * seq_len
    full_width = head_count * head_size
    return (
        grad_queries.reshape(row_total, full_width),
        grad_keys.reshape(row_total, full_width),
        grad_values.reshape(row_total, full_width),
    )


def orthogonalize(matrix):
    current = settle(matrix * lax.rsqrt(jnp.sum(matrix * matrix) + EPSILON))
    for iteration in range(NS_ITERS):
        gram_mat = settle(contract_rows(current, current))
        square = jnp.dot(gram_mat, gram_mat, preferred_element_type=jnp.float32)
        poly_mat = round_half(NEWTON_B * to_single(gram_mat) + NEWTON_C * square)
        current = settle(
            NEWTON_A * to_single(current)
            + jnp.dot(current, poly_mat, preferred_element_type=jnp.float32)
        )
    return current


def orthogonalize_attention(block_mat):
    rows_all, slot_width = block_mat.shape
    sub_blocks = jnp.transpose(block_mat.reshape(rows_all, 2, slot_width // 2), (1, 0, 2))
    solved = jnp.stack([orthogonalize(sub_blocks[which_mat]) for which_mat in range(2)])
    return jnp.transpose(solved, (1, 0, 2)).reshape(rows_all, slot_width)


def empty_block(block_mat):
    return jnp.zeros(block_mat.shape, jnp.bfloat16)


def shards(
    inputs,
    cotangent,
    norm_gains,
    attn_mats,
    router,
    expert_in,
    expert_out,
    moment_gains,
    moment_attn,
    moment_router,
    moment_in,
    moment_out,
    routes,
):
    image_count, seq_len, model_width = inputs.shape
    dp_count = lax.axis_size("dp")
    row_count = image_count * seq_len
    small_plane = jnp.zeros((1, norm_gains.shape[1], attn_mats.shape[2]), jnp.bfloat16)
    small_plane = small_plane.at[0, :, :2].set(round_half(norm_gains).T)
    small_plane = small_plane.at[0, :, 2 : 2 + EF].set(round_half(router))
    packed = lax.all_gather(
        jnp.concatenate([round_half(attn_mats), small_plane], axis=0), "dp", axis=1, tiled=True
    )
    attn_half = packed[:4]
    gains_half = packed[4, :, :2].T
    router_half = packed[4, :, 2 : 2 + EF]
    in_half = lax.all_gather(round_half(expert_in), "dp", axis=1, tiled=True)
    out_half = lax.all_gather(round_half(expert_out), "dp", axis=1, tiled=True)
    gain_one = to_single(gains_half[0])
    gain_two = to_single(gains_half[1])
    row_in = inputs.reshape(row_count, model_width)
    normal_one, inv_one, normed_one = norm_forward(row_in, gain_one)
    queries, key_rows, value_rows, log_total, attn_rows = attention_forward(
        normed_one, attn_half, image_count, seq_len
    )
    attn_part = contract_cols(attn_rows, attn_half[3])
    attn_full = lax.psum(attn_part.astype(jnp.bfloat16), "tensor").astype(jnp.float32)
    middle = row_in + attn_full
    normal_two, inv_two, normed_two = norm_forward(middle, gain_two)
    picked = routes.reshape(row_count, 2)
    one_hot = (picked[:, :, None] == jnp.arange(EF, dtype=jnp.int32)[None, None, :]).astype(
        jnp.float32
    )
    logits = jnp.dot(normed_two, router_half, preferred_element_type=jnp.float32)
    chosen = jnp.sum(logits[:, None, :] * one_hot, axis=2)
    gate_vals = jax.nn.sigmoid(chosen - chosen[:, ::-1])
    gate_table = jnp.sum(gate_vals[:, :, None] * one_hot, axis=1)
    grad_rows = cotangent.reshape(row_count, model_width)
    pre_act = jnp.einsum("td,edf->etf", normed_two, in_half, preferred_element_type=jnp.float32)
    hidden = round_half(gelu_value(pre_act))
    expert_rows = jnp.einsum("etf,edf->etd", hidden, out_half, preferred_element_type=jnp.float32)
    moe_part = jnp.sum(gate_table.T[:, :, None] * expert_rows, axis=0)
    moe_full = lax.psum(moe_part.astype(jnp.bfloat16), "tensor").astype(jnp.float32)
    output_rows = middle + moe_full
    grad_each = jnp.sum(grad_rows[None] * expert_rows, axis=2).T
    grad_choice_part = jnp.sum(grad_each[:, None, :] * one_hot, axis=2)
    grad_expert = round_half(gate_table.T[:, :, None] * grad_rows[None])
    grad_hidden = jnp.einsum(
        "etd,edf->etf", grad_expert, out_half, preferred_element_type=jnp.float32
    )
    grad_pre = round_half(grad_hidden * gelu_slope(pre_act))
    grad_normed_part = jnp.einsum(
        "etf,edf->td", grad_pre, in_half, preferred_element_type=jnp.float32
    )
    grad_in = jnp.einsum("td,etf->edf", normed_two, grad_pre, preferred_element_type=jnp.float32)
    grad_out = jnp.einsum("etd,etf->edf", grad_expert, hidden, preferred_element_type=jnp.float32)
    joined = lax.psum(
        jnp.concatenate([grad_normed_part, grad_choice_part], axis=1).astype(jnp.bfloat16), "tensor"
    ).astype(jnp.float32)
    grad_normed_moe, grad_choice = (joined[:, :model_width], joined[:, model_width:])
    gate_prod = gate_vals[:, 0] * gate_vals[:, 1]
    grad_first = (grad_choice[:, 0] - grad_choice[:, 1]) * gate_prod
    grad_picked = jnp.stack([grad_first, -grad_first], axis=1)
    grad_logits = round_half(jnp.sum(grad_picked[:, :, None] * one_hot, axis=1))
    grad_router = contract_rows(normed_two, grad_logits)
    grad_normed_two = grad_normed_moe + contract_cols(grad_logits, router_half)
    grad_mid_norm, grad_gain_two = norm_backward(grad_normed_two, normal_two, inv_two, gain_two)
    grad_middle = grad_rows + grad_mid_norm
    grad_mid_half = round_half(grad_middle)
    grad_attn_rows = round_half(
        jnp.dot(grad_mid_half, attn_half[3], preferred_element_type=jnp.float32)
    )
    grad_proj_out = contract_rows(grad_mid_half, attn_rows)
    grad_queries, grad_keys, grad_values = attention_backward(
        grad_attn_rows, queries, key_rows, value_rows, log_total
    )
    grad_attn = jnp.stack(
        [
            contract_rows(normed_one, grad_queries),
            contract_rows(normed_one, grad_keys),
            contract_rows(normed_one, grad_values),
            grad_proj_out,
        ]
    )
    grad_normed_one_part = (
        contract_cols(grad_queries, attn_half[0])
        + contract_cols(grad_keys, attn_half[1])
        + contract_cols(grad_values, attn_half[2])
    )
    grad_normed_one = lax.psum(grad_normed_one_part.astype(jnp.bfloat16), "tensor").astype(
        jnp.float32
    )
    grad_in_norm, grad_gain_one = norm_backward(grad_normed_one, normal_one, inv_one, gain_one)
    grad_inputs_rows = grad_middle + grad_in_norm
    gains_cols = jnp.stack([grad_gain_one, grad_gain_two], axis=1)
    small_cols = jnp.concatenate([gains_cols, grad_router], axis=1)
    got_attn, got_in, got_out, got_small = (
        lax.all_to_all(
            grad_attn.astype(jnp.bfloat16), "dp", split_axis=1, concat_axis=0, tiled=True
        ).astype(grad_attn.dtype),
        lax.all_to_all(
            grad_in.astype(jnp.bfloat16), "dp", split_axis=1, concat_axis=0, tiled=True
        ).astype(grad_in.dtype),
        lax.all_to_all(
            grad_out.astype(jnp.bfloat16), "dp", split_axis=1, concat_axis=0, tiled=True
        ).astype(grad_out.dtype),
        lax.all_to_all(
            small_cols[None].astype(jnp.bfloat16), "dp", split_axis=1, concat_axis=0, tiled=True
        ).astype(jnp.float32),
    )
    sum_attn = fold_sources(got_attn, dp_count)
    sum_in = fold_sources(got_in, dp_count)
    sum_out = fold_sources(got_out, dp_count)
    sum_small = fold_sources(got_small, dp_count)[0]
    sum_gains = sum_small[:, :2].T
    sum_router = sum_small[:, 2:]
    small_step = SMALL_RATE / math.sqrt(image_count * dp_count * seq_len)
    moment_gains_new = MOMENTUM * moment_gains + sum_gains
    moment_attn_new = MOMENTUM * moment_attn + sum_attn
    moment_router_new = MOMENTUM * moment_router + sum_router
    moment_in_new = MOMENTUM * moment_in + sum_in
    moment_out_new = MOMENTUM * moment_out + sum_out
    gains_new = norm_gains - small_step * moment_gains_new
    router_new = router - small_step * moment_router_new
    look_attn = sum_attn + MOMENTUM * moment_attn_new
    look_in = sum_in + MOMENTUM * moment_in_new
    look_out = sum_out + MOMENTUM * moment_out_new
    shard_rows = look_in.shape[1]
    slot_width = look_in.shape[2]
    blocks = 2 * EF + 2
    per_owner = -(-blocks // dp_count)
    slot_count = dp_count * per_owner
    slot_list = list(range(blocks))
    block_list = [
        slot_list.index(slot_number) if slot_number in slot_list else blocks
        for slot_number in range(slot_count)
    ]
    slot_of_block = np.array(slot_list)
    block_of_slot = np.array(block_list)
    kind_of_slot = np.where(block_of_slot < 2, 0, np.where(block_of_slot < blocks, 1, 2))
    attn_slots = jnp.transpose(
        jnp.transpose(look_attn, (1, 0, 2)).reshape(shard_rows, 2, slot_width), (1, 0, 2)
    )
    stacked = jnp.concatenate(
        [attn_slots, look_in, look_out, jnp.zeros((1, shard_rows, slot_width), jnp.float32)], axis=0
    )
    outgoing = jnp.take(stacked, jnp.asarray(block_of_slot, dtype=jnp.int32), axis=0)
    arrived = lax.all_to_all(
        for_sending(outgoing), "dp", split_axis=0, concat_axis=1, tiled=True
    ).astype(outgoing.dtype)
    own_index = lax.axis_index("dp")
    kind_table = jnp.asarray(kind_of_slot, dtype=jnp.int32)
    kind_now = kind_table[own_index * per_owner + 0]
    results = [
        lax.switch(kind_now, [orthogonalize_attention, orthogonalize, empty_block], arrived[0])
    ]
    finished = jnp.stack(results)
    returned = lax.all_to_all(
        for_sending(finished), "dp", split_axis=1, concat_axis=0, tiled=True
    ).astype(finished.dtype)
    updates = to_single(jnp.take(returned, jnp.asarray(slot_of_block, dtype=jnp.int32), axis=0))
    update_attn = jnp.transpose(
        jnp.transpose(updates[0:2], (1, 0, 2)).reshape(shard_rows, 4, slot_width // 2), (1, 0, 2)
    )
    attn_new = attn_mats - MUON_RATE * update_attn
    in_new = expert_in - MUON_RATE * updates[2 : EF + 2]
    out_new = expert_out - MUON_RATE * updates[EF + 2 : 2 * EF + 2]
    output = output_rows.reshape(image_count, seq_len, model_width)
    grad_inputs = grad_inputs_rows.reshape(image_count, seq_len, model_width)
    return (
        output,
        grad_inputs,
        sum_gains,
        sum_attn,
        sum_router,
        sum_in,
        sum_out,
        gains_new,
        attn_new,
        router_new,
        in_new,
        out_new,
        moment_gains_new,
        moment_attn_new,
        moment_router_new,
        moment_in_new,
        moment_out_new,
    )


def solution(mesh):
    return jax.shard_map(
        shards,
        mesh=mesh,
        in_specs=(
            P("dp", None, None),
            P("dp", None, None),
            P(None, "dp"),
            P(None, "dp", "tensor"),
            P("dp", None),
            P(None, "dp", "tensor"),
            P(None, "dp", "tensor"),
            P(None, "dp"),
            P(None, "dp", "tensor"),
            P("dp", None),
            P(None, "dp", "tensor"),
            P(None, "dp", "tensor"),
            P("dp", None, None),
        ),
        out_specs=(
            P("dp", None, None),
            P("dp", None, None),
            P(None, "dp"),
            P(None, "dp", "tensor"),
            P("dp", None),
            P(None, "dp", "tensor"),
            P(None, "dp", "tensor"),
            P(None, "dp"),
            P(None, "dp", "tensor"),
            P("dp", None),
            P(None, "dp", "tensor"),
            P(None, "dp", "tensor"),
            P(None, "dp"),
            P(None, "dp", "tensor"),
            P("dp", None),
            P(None, "dp", "tensor"),
            P(None, "dp", "tensor"),
        ),
        check_vma=False,
    )
```

profile of v0, /device:TPU:32, one launch (start us, length us, event | category | flops | bytes accessed | tf_op | source)
XLA Modules:
  0.0 853.9 jit_solution(13263834224516836586)
XLA Ops:
  9.4 2.7 and_reduce_fusion
  12.1 2.0 fusion.162
  19.4 121.1 %all-gather.4.cloned.1.call-done = bf16[5,768,192]{2,0,1:T(8,128)(2,1)} async-done(((bf16[5,12,192]{2,0,1:T(8,128)(2,1)}), bf16[5,768,192]{2,0,1:T(8,128)(2,1)}) %all-gather.4.cloned.1.call-update) | async-done | bytes 1474576 | tf_op jit(solution)/shard_map/all_gather | solution.py:191
  140.5 1.8 slice.151
  142.6 9.2 %fusion.173 = (bf16[1,768,192]{2,0,1:T(2,128)(2,1)}, bf16[1,768,192]{2,0,1:T(2,128)(2,1)}, bf16[1,768,192]{2,0,1:T(2,128)(2,1)S(1)}, bf16[1,768,192]{2,0,1:T(2,128)(2,1)S(1)}) fusion(bf16[5,768,192]{2,0,1:T(8,128)(2,1)} %all-gather.4.cloned.1.call-done), kind=kLoop, calls=%fused_computation.301 | loop fusion | bytes 2359296 | tf_op jit(solution)/shard_map/slice | solution.py:206
  151.9 2.2 copy.286
  154.7 2.2 copy.285
  166.3 2.3 slice.158
  168.9 34.6 %all-reduce.6.cloned.1.call-done = bf16[197,768]{0,1:T(8,128)(2,1)} async-done(((bf16[197,768]{0,1:T(8,128)(2,1)}), bf16[197,768]{0,1:T(8,128)(2,1)}) %all-reduce.6.cloned.1.call-update) | async-done | bytes 302608 | tf_op jit(solution)/shard_map/psum | solution.py:207
  205.4 122.8 %all-gather.6.cloned.1.call-done = bf16[3,768,384]{2,0,1:T(4,128)(2,1)} async-done(((bf16[3,12,384]{2,0,1:T(4,128)(2,1)}), bf16[3,768,384]{2,0,1:T(4,128)(2,1)}) %all-gather.6.cloned.1.call-update) | async-done | bytes 1769488 | tf_op jit(solution)/shard_map/all_gather | solution.py:197
  328.2 3.3 convolution_bitcast_fusion
  331.5 117.3 %all-gather.8.cloned.1.call-done = bf16[3,768,384]{2,0,1:T(4,128)(2,1)} async-done(((bf16[3,12,384]{2,0,1:T(4,128)(2,1)}), bf16[3,768,384]{2,0,1:T(4,128)(2,1)}) %all-gather.8.cloned.1.call-update) | async-done | bytes 1769488 | tf_op jit(solution)/shard_map/all_gather | solution.py:198
  448.8 4.0 multiply_reduce_fusion.2
  457.4 38.1 %all-reduce.8.cloned.1.call-done = bf16[197,770]{0,1:T(8,128)(2,1)} async-done(((bf16[197,770]{0,1:T(8,128)(2,1)}), bf16[197,770]{0,1:T(8,128)(2,1)}) %all-reduce.8.cloned.1.call-update) | async-done | bytes 303396 | tf_op jit(solution)/shard_map/psum | solution.py:237
  501.4 2.8 convolution_convert_fusion.17
  504.2 2.8 convolution_convert_fusion.16
  510.7 3.6 copy.251
  514.2 12.9 %all-to-all-start.1 = ((bf16[4,768,192]{2,0,1:T(4,128)(2,1)}), bf16[4,768,192]{2,0,1:T(4,128)(2,1)}, u32[]{:S(2)}, u32[]{:S(2)}) async-start(bf16[4,768,192]{2,0,1:T(4,128)(2,1)} %copy.251), calls=%async_computation.1 | async-start | bytes 3145728 | tf_op jit(solution)/shard_map/all_to_all | solution.py:278
  527.1 2.0 convert_bitcast_fusion
  529.1 5.2 copy.253
  534.3 34.5 %all-to-all-done.1 = bf16[4,768,192]{2,0,1:T(4,128)(2,1)} async-done(((bf16[4,768,192]{2,0,1:T(4,128)(2,1)}), bf16[4,768,192]{2,0,1:T(4,128)(2,1)}, u32[]{:S(2)}, u32[]{:S(2)}) %all-to-all-start.1) | async-done | bytes 1179680 | tf_op jit(solution)/shard_map/all_to_all | solution.py:278
  568.8 6.8 all-to-all-start.2
  575.6 2.1 convolution_convert_fusion.9
  577.7 2.9 copy.255
  580.7 51.8 %all-to-all-done.2 = bf16[3,768,384]{2,0,1:T(4,128)(2,1)} async-done(((bf16[3,768,384]{2,0,1:T(4,128)(2,1)}), bf16[3,768,384]{2,0,1:T(4,128)(2,1)}, u32[]{:S(2)}, u32[]{:S(2)}) %all-to-all-start.2) | async-done | bytes 1769504 | tf_op jit(solution)/shard_map/all_to_all | solution.py:281
  632.4 6.5 all-to-all-start.3
  641.3 2.3 convolution_add_fusion.11
  643.6 2.2 convert_reduce_fusion
  646.6 3.7 copy_convert_fusion.1
  650.3 4.7 reshape.538
  655.0 2.6 reduce_sum.245
  657.6 38.2 %all-to-all-done.3 = bf16[3,768,384]{2,0,1:T(4,128)(2,1)} async-done(((bf16[3,768,384]{2,0,1:T(4,128)(2,1)}), bf16[3,768,384]{2,0,1:T(4,128)(2,1)}, u32[]{:S(2)}, u32[]{:S(2)}) %all-to-all-start.3) | async-done | bytes 1769504 | tf_op jit(solution)/shard_map/all_to_all | solution.py:284
  695.7 3.7 copy_convert_fusion
  699.4 4.7 reshape.539
  704.1 2.6 reduce_sum.246
  709.2 6.4 all-to-all-start.4
  715.6 2.3 fusion.95
  723.1 41.8 %all-reduce.10.cloned.1.call-done = (bf16[197,768]{0,1:T(8,128)(2,1)}, bf16[197,768]{0,1:T(8,128)(2,1)}) async-done(((bf16[197,768]{0,1:T(8,128)(2,1)}, bf16[197,768]{0,1:T(8,128)(2,1)}), (bf16[197,768]{0,1:T(8,128)(2,1)}, bf16[197,768]{0,1:T(8,128)(2,1)})) %all-reduce.10.cloned.1.call-update) | async-done | bytes 605200 | tf_op jit(solution)/shard_map/psum | solution.py:223
  765.0 2.0 fusion.124
  768.9 12.8 %all-to-all-start = ((bf16[1,768,5]{2,0,1:T(2,128)(2,1)}), bf16[1,768,5]{2,0,1:T(2,128)(2,1)}, u32[]{:S(2)}, u32[]{:S(2)}) async-start(bf16[1,768,5]{2,0,1:T(2,128)(2,1)} %copy.249), calls=%async_computation | async-start | bytes 786432 | tf_op jit(solution)/shard_map/all_to_all | solution.py:287
  782.6 8.6 %conditional.1 = (bf16[768,384]{0,1:T(8,128)(2,1)S(1)}) conditional(s32[]{:T(128)} %bitcast.63, bf16[64,12,384]{2,1,0:T(8,128)(2,1)S(1)} %all-to-all-done.4, bf16[64,12,384]{2,1,0:T(8,128)(2,1)S(1)} %all-to-all-done.4, () %tuple.25), branch_computations={%region_28.31_spmd, %region_31.0_spmd, %region_33.34_spmd} | conditional | flops 1706655744 | bytes 14450752 | solution.py:335
  792.0 3.5 copy.259
  796.0 5.1 reduce.33
  801.1 2.6 reshape.565
  803.7 12.9 %all-to-all-start.5 = ((bf16[64,2,2304]{2,1,0:T(2,128)(2,1)}), bf16[64,2,2304]{2,1,0:T(2,128)(2,1)}, u32[]{:S(2)}, u32[]{:S(2)}) async-start(bf16[64,2,2304]{2,1,0:T(2,128)(2,1)} %reshape.565), calls=%async_computation.5 | async-start | bytes 1179648 | tf_op jit(solution)/shard_map/all_to_all | solution.py:338
  822.0 14.9 %all-to-all-done.5 = bf16[64,2,2304]{2,1,0:T(2,128)(2,1)} async-done(((bf16[64,2,2304]{2,1,0:T(2,128)(2,1)}), bf16[64,2,2304]{2,1,0:T(2,128)(2,1)}, u32[]{:S(2)}, u32[]{:S(2)}) %all-to-all-start.5) | async-done | bytes 589856 | tf_op jit(solution)/shard_map/all_to_all | solution.py:338
  836.9 3.8 reshape.566
  840.7 3.4 bitcast_reduce_fusion
  (236 shorter events, 55.4 us)
Async XLA Ops:
  7.2 9.8 %copy-start.2 = (f32[1,197,768]{2,0,1:T(1,128)S(1)}, f32[1,197,768]{2,0,1:T(1,128)}, u32[]{:S(2)}) copy-start(f32[1,197,768]{2,0,1:T(1,128)} %param.23) | copy-start | bytes 1815556
  7.2 133.3 %all-gather.4.cloned.1.call-start = ((), (), s32[]{:S(2)}) async-start(), calls=%async_computation.6 | async-start | bytes 3194880 | tf_op jit(solution)/shard_map/all_gather | solution.py:191
  15.6 187.9 %all-reduce.6.cloned.1.call-start = ((), (), s32[]{:S(2)}) async-start(), calls=%async_computation.7 | async-start | bytes 786432 | tf_op jit(solution)/shard_map/psum | solution.py:207
  154.0 9.1 %copy-start.5 = (bf16[1,768,192]{1,2,0:T(8,128)(2,1)}, bf16[1,768,192]{1,2,0:T(8,128)(2,1)S(1)}, u32[]{:S(2)}) copy-start(bf16[1,768,192]{1,2,0:T(8,128)(2,1)S(1)} %copy.286) | copy-start | bytes 884740
  156.9 4.3 copy-start.8
  161.8 4.5 copy-start.12
  163.1 5.8 copy-start.17
  164.2 164.0 %all-gather.6.cloned.1.call-start = ((), (), s32[]{:S(2)}) async-start(), calls=%async_computation.8 | async-start | bytes 2396160 | tf_op jit(solution)/shard_map/all_gather | solution.py:197
  165.0 283.8 %all-gather.8.cloned.1.call-start = ((), (), s32[]{:S(2)}) async-start(), calls=%async_computation.9 | async-start | bytes 2396160 | tf_op jit(solution)/shard_map/all_gather | solution.py:198
  165.7 329.9 %all-reduce.8.cloned.1.call-start = ((), (), s32[]{:S(2)}) async-start(), calls=%async_computation.10 | async-start | bytes 794624 | tf_op jit(solution)/shard_map/psum | solution.py:237
  166.3 286.6 %copy-start.10 = (f32[1,197,768]{2,1,0:T(8,128)}, f32[1,197,768]{2,1,0:T(8,128)S(1)}, u32[]{:S(2)}) copy-start(f32[1,197,768]{2,1,0:T(8,128)S(1)} %copy.306) | copy-start | bytes 1815556
  168.6 36.3 %copy-start.39 = (f32[768]{0:T(1024)S(1)}, f32[768]{0:T(1024)}, u32[]{:S(2)}) copy-start(f32[768]{0:T(1024)} %get-tuple-element.180) | copy-start | bytes 9220
  168.9 36.3 %copy-start.41 = (s32[1,197,2]{1,2,0:T(2,128)S(1)}, s32[1,197,2]{1,2,0:T(2,128)}, u32[]{:S(2)}) copy-start(s32[1,197,2]{1,2,0:T(2,128)} %param.35) | copy-start | bytes 4732
  204.8 291.9 %copy-start.47 = (f32[197]{0:T(256)}, f32[197]{0:T(256)S(1)}, u32[]{:S(2)}) copy-start(f32[197]{0:T(256)S(1)} %add_rsqrt_fusion) | copy-start | bytes 2368
  205.4 247.5 %copy-start.48 = (f32[197,3]{0,1:T(4,128)}, f32[197,3]{0,1:T(4,128)S(1)}, u32[]{:S(2)}) copy-start(f32[197,3]{0,1:T(4,128)S(1)} %select_reduce_fusion.2) | copy-start | bytes 7096
  448.8 4.1 copy-start.16
  448.8 4.1 copy-start.59
  500.3 6.9 copy-start.21
  514.2 12.9 %copy-start.23 = (bf16[3,197,384]{2,1,0:T(8,128)(2,1)S(1)}, bf16[3,197,384]{2,1,0:T(8,128)(2,1)}, u32[]{:S(2)}) copy-start(bf16[3,197,384]{2,1,0:T(8,128)(2,1)} %copy-done.22) | copy-start | bytes 1361668
  514.2 54.6 %all-to-all-start.1 = ((bf16[4,768,192]{2,0,1:T(4,128)(2,1)}), bf16[4,768,192]{2,0,1:T(4,128)(2,1)}, u32[]{:S(2)}, u32[]{:S(2)}) async-start(bf16[4,768,192]{2,0,1:T(4,128)(2,1)} %copy.251), calls=%async_computation.1 | async-start | bytes 3145728 | tf_op jit(solution)/shard_map/all_to_all | solution.py:278
  534.3 41.3 %copy-start.11 = (f32[1,197,768]{2,1,0:T(8,128)S(1)}, f32[1,197,768]{2,1,0:T(8,128)}, u32[]{:S(2)}) copy-start(f32[1,197,768]{2,1,0:T(8,128)} %copy-done.10) | copy-start | bytes 1815556
  534.3 41.3 %copy-start.49 = (f32[197,3]{0,1:T(4,128)S(1)}, f32[197,3]{0,1:T(4,128)}, u32[]{:S(2)}) copy-start(f32[197,3]{0,1:T(4,128)} %copy-done.48) | copy-start | bytes 7096
  568.8 63.6 %all-to-all-start.2 = ((bf16[3,768,384]{2,0,1:T(4,128)(2,1)}), bf16[3,768,384]{2,0,1:T(4,128)(2,1)}, u32[]{:S(2)}, u32[]{:S(2)}) async-start(bf16[3,768,384]{2,0,1:T(4,128)(2,1)} %copy.253), calls=%async_computation.2 | async-start | bytes 4718592 | tf_op jit(solution)/shard_map/all_to_all | solution.py:281
  580.7 58.4 %copy-start.57 = (s32[64]{0:T(128)S(1)}, s32[64]{0:T(128)}, u32[]{:S(2)}) copy-start(s32[64]{0:T(128)} %constant.199) | copy-start | bytes 772
  580.7 58.4 %copy-start.27 = (bf16[197,768]{1,0:T(8,128)(2,1)S(1)}, bf16[197,768]{1,0:T(8,128)(2,1)}, u32[]{:S(2)}) copy-start(bf16[197,768]{1,0:T(8,128)(2,1)} %get-tuple-element.173) | copy-start | bytes 907780
  632.4 63.3 %all-to-all-start.3 = ((bf16[3,768,384]{2,0,1:T(4,128)(2,1)}), bf16[3,768,384]{2,0,1:T(4,128)(2,1)}, u32[]{:S(2)}, u32[]{:S(2)}) async-start(bf16[3,768,384]{2,0,1:T(4,128)(2,1)} %copy.255), calls=%async_computation.3 | async-start | bytes 4718592 | tf_op jit(solution)/shard_map/all_to_all | solution.py:284
  641.3 4.5 copy-start.40
  645.8 4.4 copy-start.34
  657.6 49.2 %copy-start.32 = (f32[3,12,384]{2,1,0:T(8,128)}, f32[3,12,384]{2,1,0:T(8,128)S(1)}, u32[]{:S(2)}) copy-start(f32[3,12,384]{2,1,0:T(8,128)S(1)} %reduce_sum.245) | copy-start | bytes 165892
  709.2 59.7 %all-to-all-start.4 = ((bf16[64,12,384]{2,1,0:T(8,128)(2,1)}), bf16[64,12,384]{2,1,0:T(8,128)(2,1)S(1)}, u32[]{:S(2)}, u32[]{:S(2)}) async-start(bf16[64,12,384]{2,1,0:T(8,128)(2,1)} %gather_fusion), calls=%async_computation.4 | async-start | bytes 1572864 | tf_op jit(solution)/shard_map/all_to_all | solution.py:328
  715.5 49.4 %copy-start.38 = (f32[768]{0:T(1024)S(1)}, f32[768]{0:T(1024)}, u32[]{:S(2)}) copy-start(f32[768]{0:T(1024)} %get-tuple-element.181) | copy-start | bytes 9220
  715.6 49.4 %copy-start.43 = (f32[197]{0:T(256)S(1)}, f32[197]{0:T(256)}, u32[]{:S(2)}) copy-start(f32[197]{0:T(256)} %copy-done.42) | copy-start | bytes 2368
  715.6 49.4 %copy-start.45 = (f32[197]{0:T(256)S(1)}, f32[197]{0:T(256)}, u32[]{:S(2)}) copy-start(f32[197]{0:T(256)} %add_rsqrt_fusion.1) | copy-start | bytes 2368
  715.6 49.4 %all-reduce.10.cloned.1.call-start = ((), (), s32[]{:S(2)}) async-start(), calls=%async_computation.11 | async-start | bytes 1572864 | tf_op jit(solution)/shard_map/psum | solution.py:223
  765.0 16.7 %copy-start.26 = (bf16[197,768]{0,1:T(8,128)(2,1)S(1)}, bf16[197,768]{0,1:T(8,128)(2,1)}, u32[]{:S(2)}) copy-start(bf16[197,768]{0,1:T(8,128)(2,1)} %get-tuple-element.182) | copy-start | bytes 907780
  768.9 34.9 %all-to-all-start = ((bf16[1,768,5]{2,0,1:T(2,128)(2,1)}), bf16[1,768,5]{2,0,1:T(2,128)(2,1)}, u32[]{:S(2)}, u32[]{:S(2)}) async-start(bf16[1,768,5]{2,0,1:T(2,128)(2,1)} %copy.249), calls=%async_computation | async-start | bytes 786432 | tf_op jit(solution)/shard_map/all_to_all | solution.py:287
  796.0 20.6 %copy-start.52 = (f32[197]{0:T(256)S(1)}, f32[197]{0:T(256)}, u32[]{:S(2)}) copy-start(f32[197]{0:T(256)} %get-tuple-element.177) | copy-start | bytes 2368
  801.1 15.6 %copy-start.3 = (f32[1,197,768]{1,2,0:T(8,128)S(1)}, f32[1,197,768]{1,2,0:T(8,128)}, u32[]{:S(2)}) copy-start(f32[1,197,768]{1,2,0:T(8,128)} %add_bitcast_fusion) | copy-start | bytes 1815556
  801.1 16.7 %copy-start.51 = (f32[197]{0:T(256)S(1)}, f32[197]{0:T(256)}, u32[]{:S(2)}) copy-start(f32[197]{0:T(256)} %get-tuple-element.179) | copy-start | bytes 2368
  801.1 16.7 %copy-start.15 = (bf16[197,768]{0,1:T(8,128)(2,1)S(1)}, bf16[197,768]{0,1:T(8,128)(2,1)}, u32[]{:S(2)}) copy-start(bf16[197,768]{0,1:T(8,128)(2,1)} %get-tuple-element.183) | copy-start | bytes 907780
  801.1 16.7 %copy-start.44 = (f32[197]{0:T(256)S(1)}, f32[197]{0:T(256)}, u32[]{:S(2)}) copy-start(f32[197]{0:T(256)} %copy-done.42) | copy-start | bytes 2368
  801.1 16.7 %copy-start.46 = (f32[197]{0:T(256)S(1)}, f32[197]{0:T(256)}, u32[]{:S(2)}) copy-start(f32[197]{0:T(256)} %add_rsqrt_fusion.1) | copy-start | bytes 2368
  803.7 33.1 %all-to-all-start.5 = ((bf16[64,2,2304]{2,1,0:T(2,128)(2,1)}), bf16[64,2,2304]{2,1,0:T(2,128)(2,1)}, u32[]{:S(2)}, u32[]{:S(2)}) async-start(bf16[64,2,2304]{2,1,0:T(2,128)(2,1)} %reshape.565), calls=%async_computation.5 | async-start | bytes 1179648 | tf_op jit(solution)/shard_map/all_to_all | solution.py:338
  818.1 3.3 copy-start.50
  840.7 4.3 copy-start.56
  840.7 4.4 copy-start.29
  840.7 4.4 copy-start.31
  840.7 5.3 copy-start.35
  (24 other events, 46.0 us)
Sparse Core Ops, SparseCore 0:
  15.7 124.7 all-gather.3
  164.4 39.1 all-reduce.5
  208.4 119.7 all-gather.5
  332.9 115.8 all-gather.7
  456.3 39.2 all-reduce.7
  719.4 45.5 all-reduce.9
where the time goes:
time: 861 us; the launch traced here: 854 us
  waiting for transfers between devices  615 us (71%)
  local copies, waits for them, and re-layouts  75.5 us (9%)
  starting transfers between devices  59 us (7%)
  other arithmetic  45.9 us (5%)
  matrix products  33.5 us (4%)
  between operations  16.3 us (2%)
    all_gather x1, waiting for transfers between devices, shards(): in_half = lax.all_gather(round_half(expert_in), 'dp', axis=1, tiled=True)  123 us
    all_gather x1, waiting for transfers between devices, shards(): lax.all_gather(jnp.concatenate([round_half(attn_mats), small_plane], axis...  121 us
    all_gather x1, waiting for transfers between devices, shards(): out_half = lax.all_gather(round_half(expert_out), 'dp', axis=1, tiled=True)  117 us
    all_to_all x1, waiting for transfers between devices, shards(): lax.all_to_all(grad_in.astype(jnp.bfloat16), 'dp', split_axis=1, concat_a...  51.8 us
    psum x1, waiting for transfers between devices, shards(): lax.psum(moe_part.astype(jnp.bfloat16), 'tensor').astype(jnp.float32)  41.8 us
    all_to_all x1, waiting for transfers between devices, shards(): lax.all_to_all(grad_out.astype(jnp.bfloat16), 'dp', split_axis=1, concat_...  38.2 us
    psum x1, waiting for transfers between devices, shards(): lax.psum(jnp.concatenate([grad_normed_part, grad_choice_part], axis=1).as...  38.1 us
    psum x1, waiting for transfers between devices, shards(): lax.psum(attn_part.astype(jnp.bfloat16), 'tensor').astype(jnp.float32)  34.6 us
  transfers between devices with their start and end apart: 12, of which 10 were waited for; matrix products, arithmetic and copies ran while one was open for 9% of the time, Pallas kernels for 0%

commit v1 on v0

--- a/solution.py
+++ b/solution.py
@@ -275,8 +275,14 @@
     gains_cols = jnp.stack([grad_gain_one, grad_gain_two], axis=1)
     small_cols = jnp.concatenate([gains_cols, grad_router], axis=1)
     got_attn, got_in, got_out, got_small = (
-        lax.all_to_all(
-            grad_attn.astype(jnp.bfloat16), "dp", split_axis=1, concat_axis=0, tiled=True
+        jnp.concatenate(
+            lax.all_to_all(
+                jnp.stack(jnp.split(grad_attn.astype(jnp.bfloat16), lax.axis_size("dp"), axis=1)),
+                "dp",
+                0,
+                0,
+            ),
+            axis=0,
         ).astype(grad_attn.dtype),
         lax.all_to_all(
             grad_in.astype(jnp.bfloat16), "dp", split_axis=1, concat_axis=0, tiled=True

time: 861 us -> 940 us (1.092)
  local copies, waits for them, and re-layouts: 75.5 us -> 134 us
  starting transfers between devices: 59 us -> 76.4 us
    unnamed x134 -> x148, local copies, waits for them, and re-layouts: 23.2 us -> 71 us
    all_to_all x1, starting transfers between devices: 6.78 us -> 16.6 us  [shards(): lax.all_to_all(grad_in.astype(jnp.bfloat16), 'dp', split_axis=1, concat_a...]
  transfers between devices with their start and end apart: 12 -> 12, of which waited for: 10 -> 11; matrix products, arithmetic and copies ran while one was open for 9% -> 9% of each run, Pallas kernels for 0% -> 0%
where the time goes in v1:
time: 940 us; the launch traced here: 929 us
  waiting for transfers between devices  608 us (65%)
  local copies, waits for them, and re-layouts  134 us (14%)
  starting transfers between devices  76.4 us (8%)
  other arithmetic  52.1 us (6%)
  matrix products  42.7 us (5%)
  between operations  16.1 us (2%)
    all_gather x1, waiting for transfers between devices, shards(): in_half = lax.all_gather(round_half(expert_in), 'dp', axis=1, tiled=True)  123 us
    all_gather x1, waiting for transfers between devices, shards(): lax.all_gather(jnp.concatenate([round_half(attn_mats), small_plane], axis...  121 us
    all_gather x1, waiting for transfers between devices, shards(): out_half = lax.all_gather(round_half(expert_out), 'dp', axis=1, tiled=True)  117 us
    unnamed x148, local copies, waits for them, and re-layouts  71 us
    all_to_all x1, waiting for transfers between devices, shards(): lax.all_to_all(grad_in.astype(jnp.bfloat16), 'dp', split_axis=1, concat_a...  51.6 us
    psum x1, waiting for transfers between devices, shards(): lax.psum(moe_part.astype(jnp.bfloat16), 'tensor').astype(jnp.float32)  43.1 us
    psum x1, waiting for transfers between devices, shards(): lax.psum(jnp.concatenate([grad_normed_part, grad_choice_part], axis=1).as...  37.1 us
    all_to_all x1, waiting for transfers between devices, shards(): lax.all_to_all(grad_out.astype(jnp.bfloat16), 'dp', split_axis=1, concat_...  34.1 us
  transfers between devices with their start and end apart: 12, of which 11 were waited for; matrix products, arithmetic and copies ran while one was open for 9% of the time, Pallas kernels for 0%

profile of v1, /device:TPU:32, one launch (start us, length us, event | category | flops | bytes accessed | tf_op | source)
XLA Modules:
  0.0 928.8 jit_solution(17215878948423739907)
XLA Ops:
  9.4 2.7 and_reduce_fusion
  17.0 2.1 reduce_sum.225
  19.3 121.2 %all-gather.4.cloned.1.call-done = bf16[5,768,192]{2,0,1:T(8,128)(2,1)} async-done(((bf16[5,12,192]{2,0,1:T(8,128)(2,1)}), bf16[5,768,192]{2,0,1:T(8,128)(2,1)}) %all-gather.4.cloned.1.call-update) | async-done | bytes 1474576 | tf_op jit(solution)/shard_map/all_gather | solution.py:191
  142.7 9.2 fusion.237
  151.9 2.2 copy.447
  154.1 2.9 copy.446
  168.2 2.1 slice.158
  170.6 33.4 %all-reduce.6.cloned.1.call-done = bf16[197,768]{0,1:T(8,128)(2,1)} async-done(((bf16[197,768]{0,1:T(8,128)(2,1)}), bf16[197,768]{0,1:T(8,128)(2,1)}) %all-reduce.6.cloned.1.call-update) | async-done | bytes 302608 | tf_op jit(solution)/shard_map/psum | solution.py:207
  205.9 122.8 %all-gather.6.cloned.1.call-done = bf16[3,768,384]{2,0,1:T(4,128)(2,1)} async-done(((bf16[3,12,384]{2,0,1:T(4,128)(2,1)}), bf16[3,768,384]{2,0,1:T(4,128)(2,1)}) %all-gather.6.cloned.1.call-update) | async-done | bytes 1769488 | tf_op jit(solution)/shard_map/all_gather | solution.py:197
  328.7 3.2 convolution_bitcast_fusion
  331.9 117.4 %all-gather.8.cloned.1.call-done = bf16[3,768,384]{2,0,1:T(4,128)(2,1)} async-done(((bf16[3,12,384]{2,0,1:T(4,128)(2,1)}), bf16[3,768,384]{2,0,1:T(4,128)(2,1)}) %all-gather.8.cloned.1.call-update) | async-done | bytes 1769488 | tf_op jit(solution)/shard_map/all_gather | solution.py:198
  449.3 3.9 multiply_reduce_fusion.2
  453.3 2.9 fusion.86
  456.2 2.5 fusion.96
  459.6 2.3 copy.389
  461.9 37.1 %all-reduce.8.cloned.1.call-done = bf16[197,770]{0,1:T(8,128)(2,1)} async-done(((bf16[197,770]{0,1:T(8,128)(2,1)}), bf16[197,770]{0,1:T(8,128)(2,1)}) %all-reduce.8.cloned.1.call-update) | async-done | bytes 303396 | tf_op jit(solution)/shard_map/psum | solution.py:237
  506.6 2.1 fusion.240
  508.6 2.2 convolution_convert_fusion.17
  510.8 2.9 convolution_convert_fusion.16
  567.4 11.9 %copy.403 = bf16[64,4,12,192]{3,1,2,0:T(4,128)(2,1)} copy(bf16[64,4,12,192]{2,3,1,0:T(8,128)(2,1)} %fusion.150) | data formatting | bytes 2359296 | tf_op jit(solution)/shard_map/stack | solution.py:280
  579.4 12.8 %all-to-all-start.1 = ((bf16[64,4,12,192]{3,1,2,0:T(4,128)(2,1)}), bf16[64,4,12,192]{3,1,2,0:T(4,128)(2,1)}, u32[]{:S(2)}, u32[]{:S(2)}) async-start(bf16[64,4,12,192]{3,1,2,0:T(4,128)(2,1)} %copy.403), calls=%async_computation.1 | async-start | bytes 3145728 | tf_op jit(solution)/shard_map/all_to_all | solution.py:279
  592.2 3.0 convert_bitcast_fusion
  595.2 5.2 copy.407
  600.4 33.4 %all-to-all-done.1 = bf16[64,4,12,192]{3,1,2,0:T(4,128)(2,1)} async-done(((bf16[64,4,12,192]{3,1,2,0:T(4,128)(2,1)}), bf16[64,4,12,192]{3,1,2,0:T(4,128)(2,1)}, u32[]{:S(2)}, u32[]{:S(2)}) %all-to-all-start.1) | async-done | bytes 1179680 | tf_op jit(solution)/shard_map/all_to_all | solution.py:279
  633.8 16.6 %all-to-all-start.2 = ((bf16[3,768,384]{2,0,1:T(4,128)(2,1)}), bf16[3,768,384]{2,0,1:T(4,128)(2,1)}, u32[]{:S(2)}, u32[]{:S(2)}) async-start(bf16[3,768,384]{2,0,1:T(4,128)(2,1)} %copy.407), calls=%async_computation.2 | async-start | bytes 4718592 | tf_op jit(solution)/shard_map/all_to_all | solution.py:287
  650.4 2.3 convolution_convert_fusion.9
  652.7 2.9 copy.409
  655.6 51.6 %all-to-all-done.2 = bf16[3,768,384]{2,0,1:T(4,128)(2,1)} async-done(((bf16[3,768,384]{2,0,1:T(4,128)(2,1)}), bf16[3,768,384]{2,0,1:T(4,128)(2,1)}, u32[]{:S(2)}, u32[]{:S(2)}) %all-to-all-start.2) | async-done | bytes 1769504 | tf_op jit(solution)/shard_map/all_to_all | solution.py:287
  707.2 6.5 all-to-all-start.3
  718.5 2.2 convolution_add_fusion.11
  720.6 2.0 convert_reduce_fusion
  725.4 3.7 copy_convert_fusion.1
  729.1 4.7 reshape.536
  733.8 2.6 reduce_sum.245
  736.5 34.1 %all-to-all-done.3 = bf16[3,768,384]{2,0,1:T(4,128)(2,1)} async-done(((bf16[3,768,384]{2,0,1:T(4,128)(2,1)}), bf16[3,768,384]{2,0,1:T(4,128)(2,1)}, u32[]{:S(2)}, u32[]{:S(2)}) %all-to-all-start.3) | async-done | bytes 1769504 | tf_op jit(solution)/shard_map/all_to_all | solution.py:290
  770.6 3.7 copy_convert_fusion
  774.2 4.7 reshape.537
  778.9 2.6 reduce_sum.246
  783.9 6.4 all-to-all-start.4
  790.3 2.3 fusion.95
  796.6 43.1 %all-reduce.10.cloned.1.call-done = (bf16[197,768]{0,1:T(8,128)(2,1)}, bf16[197,768]{0,1:T(8,128)(2,1)}) async-done(((bf16[197,768]{0,1:T(8,128)(2,1)}, bf16[197,768]{0,1:T(8,128)(2,1)}), (bf16[197,768]{0,1:T(8,128)(2,1)}, bf16[197,768]{0,1:T(8,128)(2,1)})) %all-reduce.10.cloned.1.call-update) | async-done | bytes 605200 | tf_op jit(solution)/shard_map/psum | solution.py:223
  843.4 12.6 %all-to-all-start = ((bf16[1,768,5]{2,0,1:T(2,128)(2,1)}), bf16[1,768,5]{2,0,1:T(2,128)(2,1)S(1)}, u32[]{:S(2)}, u32[]{:S(2)}) async-start(bf16[1,768,5]{2,0,1:T(2,128)(2,1)} %copy.401), calls=%async_computation | async-start | bytes 786432 | tf_op jit(solution)/shard_map/all_to_all | solution.py:293
  858.3 2.8 copy.416
  861.6 5.2 reduce.32
  867.8 5.2 all-to-all-done
  873.0 21.2 %all-to-all-start.5 = ((bf16[64,2,2304]{2,1,0:T(2,128)(2,1)}), bf16[64,2,2304]{2,1,0:T(2,128)(2,1)S(1)}, u32[]{:S(2)}, u32[]{:S(2)}) async-start(bf16[64,2,2304]{2,1,0:T(2,128)(2,1)} %reshape.563), calls=%async_computation.5 | async-start | bytes 1179648 | tf_op jit(solution)/shard_map/all_to_all | solution.py:344
  906.2 8.3 all-to-all-done.5
  914.9 3.4 bitcast_reduce_fusion
  (252 shorter events, 120.6 us)
Async XLA Ops:
  7.2 151.9 %copy-start.1 = (f32[1,197,768]{2,0,1:T(1,128)S(1)}, f32[1,197,768]{2,0,1:T(1,128)}, u32[]{:S(2)}) copy-start(f32[1,197,768]{2,0,1:T(1,128)} %param.23) | copy-start | bytes 1815556
  7.2 157.6 %copy-start.13 = (f32[3,12,384]{2,1,0:T(8,128)S(1)}, f32[3,12,384]{2,1,0:T(8,128)}, u32[]{:S(2)}) copy-start(f32[3,12,384]{2,1,0:T(8,128)} %param.28) | copy-start | bytes 165892
  7.2 158.3 %copy-start.15 = (f32[3,12,384]{2,1,0:T(8,128)S(1)}, f32[3,12,384]{2,1,0:T(8,128)}, u32[]{:S(2)}) copy-start(f32[3,12,384]{2,1,0:T(8,128)} %param.29) | copy-start | bytes 165892
  7.2 133.3 %all-gather.4.cloned.1.call-start = ((), (), s32[]{:S(2)}) async-start(), calls=%async_computation.6 | async-start | bytes 3194880 | tf_op jit(solution)/shard_map/all_gather | solution.py:191
  15.6 188.4 %all-reduce.6.cloned.1.call-start = ((), (), s32[]{:S(2)}) async-start(), calls=%async_computation.7 | async-start | bytes 786432 | tf_op jit(solution)/shard_map/psum | solution.py:207
  19.2 143.8 %copy-start.23 = (f32[197]{0:T(256)}, f32[197]{0:T(256)S(1)}, u32[]{:S(2)}) copy-start(f32[197]{0:T(256)S(1)} %broadcast_multiply_fusion.6) | copy-start | bytes 2368
  19.3 186.0 %copy-start.27 = (f32[197]{0:T(256)}, f32[197]{0:T(256)S(1)}, u32[]{:S(2)}) copy-start(f32[197]{0:T(256)S(1)} %add_rsqrt_fusion.1) | copy-start | bytes 2368
  142.7 63.0 %copy-start.22 = (s32[1,197,2]{1,2,0:T(2,128)S(1)}, s32[1,197,2]{1,2,0:T(2,128)}, u32[]{:S(2)}) copy-start(s32[1,197,2]{1,2,0:T(2,128)} %param.35) | copy-start | bytes 4732
  154.0 51.3 %copy-start.3 = (bf16[1,768,192]{1,2,0:T(8,128)(2,1)}, bf16[1,768,192]{1,2,0:T(8,128)(2,1)S(1)}, u32[]{:S(2)}) copy-start(bf16[1,768,192]{1,2,0:T(8,128)(2,1)S(1)} %copy.447) | copy-start | bytes 884740
  159.1 297.1 %copy-start.5 = (bf16[1,768,192]{1,2,0:T(8,128)(2,1)}, bf16[1,768,192]{1,2,0:T(8,128)(2,1)S(1)}, u32[]{:S(2)}) copy-start(bf16[1,768,192]{1,2,0:T(8,128)(2,1)S(1)} %copy.444) | copy-start | bytes 884740
  161.4 2.0 copy-start.11
  161.7 4.6 copy-start.12
  162.9 3.3 copy-start.8
  163.3 7.3 copy-start
  163.7 6.9 copy-start.7
  164.8 164.0 %all-gather.6.cloned.1.call-start = ((), (), s32[]{:S(2)}) async-start(), calls=%async_computation.8 | async-start | bytes 2396160 | tf_op jit(solution)/shard_map/all_gather | solution.py:197
  165.5 283.8 %all-gather.8.cloned.1.call-start = ((), (), s32[]{:S(2)}) async-start(), calls=%async_computation.9 | async-start | bytes 2396160 | tf_op jit(solution)/shard_map/all_gather | solution.py:198
  166.2 332.8 %all-reduce.8.cloned.1.call-start = ((), (), s32[]{:S(2)}) async-start(), calls=%async_computation.10 | async-start | bytes 794624 | tf_op jit(solution)/shard_map/psum | solution.py:237
  205.2 295.5 %copy-start.25 = (f32[197]{0:T(256)}, f32[197]{0:T(256)S(1)}, u32[]{:S(2)}) copy-start(f32[197]{0:T(256)S(1)} %broadcast_multiply_fusion.5) | copy-start | bytes 2368
  205.4 295.3 %copy-start.29 = (f32[197]{0:T(256)}, f32[197]{0:T(256)S(1)}, u32[]{:S(2)}) copy-start(f32[197]{0:T(256)S(1)} %add_rsqrt_fusion) | copy-start | bytes 2368
  205.9 294.8 %copy-start.30 = (f32[197,3]{0,1:T(4,128)}, f32[197,3]{0,1:T(4,128)S(1)}, u32[]{:S(2)}) copy-start(f32[197,3]{0,1:T(4,128)S(1)} %select_reduce_fusion.2) | copy-start | bytes 7096
  456.2 5.7 copy-start.10
  500.1 0.6 copy-start.26
  567.4 83.0 %copy-start.31 = (f32[197,3]{0,1:T(4,128)S(1)}, f32[197,3]{0,1:T(4,128)}, u32[]{:S(2)}) copy-start(f32[197,3]{0,1:T(4,128)} %copy-done.30) | copy-start | bytes 7096
  579.4 54.4 %all-to-all-start.1 = ((bf16[64,4,12,192]{3,1,2,0:T(4,128)(2,1)}), bf16[64,4,12,192]{3,1,2,0:T(4,128)(2,1)}, u32[]{:S(2)}, u32[]{:S(2)}) async-start(bf16[64,4,12,192]{3,1,2,0:T(4,128)(2,1)} %copy.403), calls=%async_computation.1 | async-start | bytes 3145728 | tf_op jit(solution)/shard_map/all_to_all | solution.py:279
  592.2 123.5 %copy-start.33 = (s32[64]{0:T(128)S(1)}, s32[64]{0:T(128)}, u32[]{:S(2)}) copy-start(s32[64]{0:T(128)} %constant.199) | copy-start | bytes 772
  592.2 126.0 %copy-start.4 = (bf16[1,768,192]{1,2,0:T(8,128)(2,1)S(1)}, bf16[1,768,192]{1,2,0:T(8,128)(2,1)}, u32[]{:S(2)}) copy-start(bf16[1,768,192]{1,2,0:T(8,128)(2,1)} %copy.445) | copy-start | bytes 884740
  592.2 126.3 %copy-start.6 = (bf16[1,768,192]{1,2,0:T(8,128)(2,1)S(1)}, bf16[1,768,192]{1,2,0:T(8,128)(2,1)}, u32[]{:S(2)}) copy-start(bf16[1,768,192]{1,2,0:T(8,128)(2,1)} %copy-done.5) | copy-start | bytes 884740
  633.8 73.4 %all-to-all-start.2 = ((bf16[3,768,384]{2,0,1:T(4,128)(2,1)}), bf16[3,768,384]{2,0,1:T(4,128)(2,1)}, u32[]{:S(2)}, u32[]{:S(2)}) async-start(bf16[3,768,384]{2,0,1:T(4,128)(2,1)} %copy.407), calls=%async_computation.2 | async-start | bytes 4718592 | tf_op jit(solution)/shard_map/all_to_all | solution.py:287
  707.2 63.3 %all-to-all-start.3 = ((bf16[3,768,384]{2,0,1:T(4,128)(2,1)}), bf16[3,768,384]{2,0,1:T(4,128)(2,1)}, u32[]{:S(2)}, u32[]{:S(2)}) async-start(bf16[3,768,384]{2,0,1:T(4,128)(2,1)} %copy.409), calls=%async_computation.3 | async-start | bytes 4718592 | tf_op jit(solution)/shard_map/all_to_all | solution.py:290
  722.7 0.6 copy-start.9
  733.8 47.7 %copy-start.20 = (f32[3,12,384]{2,1,0:T(8,128)S(1)}, f32[3,12,384]{2,1,0:T(8,128)}, u32[]{:S(2)}) copy-start(f32[3,12,384]{2,1,0:T(8,128)} %param.34) | copy-start | bytes 165892
  733.8 47.7 %copy-start.21 = (f32[3,12,384]{2,1,0:T(8,128)S(1)}, f32[3,12,384]{2,1,0:T(8,128)}, u32[]{:S(2)}) copy-start(f32[3,12,384]{2,1,0:T(8,128)} %param.33) | copy-start | bytes 165892
  736.4 45.8 %copy-start.17 = (f32[3,12,384]{2,1,0:T(8,128)}, f32[3,12,384]{2,1,0:T(8,128)S(1)}, u32[]{:S(2)}) copy-start(f32[3,12,384]{2,1,0:T(8,128)S(1)} %reduce_sum.245) | copy-start | bytes 165892
  736.4 103.2 %copy-start.24 = (f32[197]{0:T(256)S(1)}, f32[197]{0:T(256)}, u32[]{:S(2)}) copy-start(f32[197]{0:T(256)} %copy-done.23) | copy-start | bytes 2368
  781.5 0.7 copy-start.18
  783.9 59.6 %all-to-all-start.4 = ((bf16[64,12,384]{2,1,0:T(8,128)(2,1)}), bf16[64,12,384]{2,1,0:T(8,128)(2,1)S(1)}, u32[]{:S(2)}, u32[]{:S(2)}) async-start(bf16[64,12,384]{2,1,0:T(8,128)(2,1)} %gather_fusion), calls=%async_computation.4 | async-start | bytes 1572864 | tf_op jit(solution)/shard_map/all_to_all | solution.py:334
  790.2 49.4 %all-reduce.10.cloned.1.call-start = ((), (), s32[]{:S(2)}) async-start(), calls=%async_computation.11 | async-start | bytes 1572864 | tf_op jit(solution)/shard_map/psum | solution.py:223
  843.4 29.6 %all-to-all-start = ((bf16[1,768,5]{2,0,1:T(2,128)(2,1)}), bf16[1,768,5]{2,0,1:T(2,128)(2,1)S(1)}, u32[]{:S(2)}, u32[]{:S(2)}) async-start(bf16[1,768,5]{2,0,1:T(2,128)(2,1)} %copy.401), calls=%async_computation | async-start | bytes 786432 | tf_op jit(solution)/shard_map/all_to_all | solution.py:293
  858.0 37.5 %copy-start.2 = (f32[1,197,768]{1,2,0:T(8,128)S(1)}, f32[1,197,768]{1,2,0:T(8,128)}, u32[]{:S(2)}) copy-start(f32[1,197,768]{1,2,0:T(8,128)} %add_bitcast_fusion) | copy-start | bytes 1815556
  858.0 39.3 %copy-start.28 = (f32[197]{0:T(256)S(1)}, f32[197]{0:T(256)}, u32[]{:S(2)}) copy-start(f32[197]{0:T(256)} %copy-done.27) | copy-start | bytes 2368
  858.0 43.6 %copy-start.32 = (f32[12,3]{0,1:T(4,128)S(1)}, f32[12,3]{0,1:T(4,128)}, u32[]{:S(2)}) copy-start(f32[12,3]{0,1:T(4,128)} %param.27) | copy-start | bytes 436
  858.3 61.7 %copy-start.14 = (f32[3,12,384]{2,1,0:T(8,128)S(1)}, f32[3,12,384]{2,1,0:T(8,128)}, u32[]{:S(2)}) copy-start(f32[3,12,384]{2,1,0:T(8,128)} %param.28) | copy-start | bytes 165892
  858.3 61.7 %copy-start.16 = (f32[3,12,384]{2,1,0:T(8,128)S(1)}, f32[3,12,384]{2,1,0:T(8,128)}, u32[]{:S(2)}) copy-start(f32[3,12,384]{2,1,0:T(8,128)} %param.29) | copy-start | bytes 165892
  858.3 62.5 %copy-start.19 = (f32[4,12,192]{2,0,1:T(4,128)S(1)}, f32[4,12,192]{2,0,1:T(4,128)}, u32[]{:S(2)}) copy-start(f32[4,12,192]{2,0,1:T(4,128)} %param.26) | copy-start | bytes 110596
  873.0 41.4 %all-to-all-start.5 = ((bf16[64,2,2304]{2,1,0:T(2,128)(2,1)}), bf16[64,2,2304]{2,1,0:T(2,128)(2,1)S(1)}, u32[]{:S(2)}, u32[]{:S(2)}) async-start(bf16[64,2,2304]{2,1,0:T(2,128)(2,1)} %reshape.563), calls=%async_computation.5 | async-start | bytes 1179648 | tf_op jit(solution)/shard_map/all_to_all | solution.py:344
Sparse Core Ops, SparseCore 0:
  15.8 124.7 all-gather.3
  164.9 39.1 all-reduce.5
  208.9 119.7 all-gather.5
  333.4 115.8 all-gather.7
  459.7 39.2 all-reduce.7
  794.1 45.5 all-reduce.9
